TPU v7x, 32 devices: a whole 2x2x4 slice. The times are simulated.
32 devices in a mesh: row: 2 (over y), col: 8 (over z, core), orient: 2 (over x).
Axes of the slice: x: 2, y: 2, z: 4, core: 2. Of those that a mesh axis runs over, the one named last changes fastest.
Arguments:
- noise: float32 [2, 4096, 4096], P(None, ('row', 'col')), may hold values from -6 to 6
- elevation_library: float32 [16, 128, 128], replicated, may hold values from 0.25 to 1
- tile_choice_index: int32 [32, 32], P('row', 'col'), may hold values from 0 to 15
- family_heading_index: int32 [8], P('orient'), may hold values from 0 to 35
- family_extent_index: int32 [8], P('orient'), may hold values from 0 to 3
Outputs:
- safety_min: float32 [4096, 4096], P('row', ('col', 'orient'))
All inputs are finite; a program needn't handle non-finite values.
Results may differ from a plain program's by a relative error of at most 0.0005.
Values may be sent and summed in bfloat16 or wider, within the bound.
A program may use at most 256 MiB of HBM per device.

v0:
```python
import math
import jax
import jax.numpy as jnp
from jax import lax
from jax.sharding import PartitionSpec as P

R = 8
N_AZ = 36
NSIZE = 4
nugget_share = 0.3
peak_share = 1024.0 / (2.0 * math.pi)
cutoff_ratio = 32.0


def extended(cells, sides, width):
    for axis, dim in sides:
        count = lax.axis_size(axis)
        ends = count - 1
        head = lax.slice_in_dim(cells, 0, width, axis=dim)
        tail = lax.slice_in_dim(cells, cells.shape[dim] - width, cells.shape[dim], axis=dim)
        cells = jnp.concatenate(
            [
                lax.ppermute(tail, axis, [(i, (i + 1) % count) for i in range(ends)]),
                cells,
                lax.ppermute(head, axis, [((i + 1) % count, i) for i in range(ends)]),
            ],
            axis=dim,
        )
    return cells


def partner(x, axis, bit):
    return lax.ppermute(x, axis, [(i, i ^ 1 << bit) for i in range(lax.axis_size(axis))])


def amplitude(u_index, v_index, side_cells):
    wrap_u = jnp.minimum(u_index, side_cells - u_index).astype(jnp.float32)
    wrap_v = jnp.minimum(v_index, side_cells - v_index).astype(jnp.float32)
    cutoff = side_cells / cutoff_ratio
    scaled_u = wrap_u / cutoff
    scaled_v = wrap_v / cutoff
    grown = 1.0 + scaled_u * scaled_u + scaled_v * scaled_v
    spectrum = nugget_share + peak_share / (grown * jnp.sqrt(grown))
    return jnp.sqrt(spectrum) / side_cells


def ellipsoid(offset_u, offset_v, azimuth, size_index):
    heading = azimuth.astype(jnp.float32) * (math.pi / N_AZ)
    semi_axis = R * (size_index.astype(jnp.float32) + (1 + NSIZE)) / (2 * NSIZE)
    across = 0.6 * semi_axis
    slip_depth = 0.3 * semi_axis
    along = offset_u * jnp.cos(heading) + offset_v * jnp.sin(heading)
    lateral = offset_v * jnp.cos(heading) - offset_u * jnp.sin(heading)
    along_part = along / semi_axis
    lateral_part = lateral / across
    inside = 1.0 - along_part * along_part - lateral_part * lateral_part
    height = slip_depth * jnp.sqrt(jnp.maximum(inside, 0.0))
    base_share = jnp.clip(4.0 * inside, 0.0, 1.0)
    return (height, base_share)


def angle_table(row_count, col_count, period):
    left_index = lax.broadcasted_iota(jnp.int32, (row_count, col_count), 0)
    right_index = lax.broadcasted_iota(jnp.int32, (row_count, col_count), 1)
    phase_step = left_index * right_index % period
    angles = phase_step.astype(jnp.float32) * (2.0 * math.pi / period)
    return (jnp.cos(angles), jnp.sin(angles))


def transform_last(real_part, imag_part):
    length = real_part.shape[-1]
    inner_size = 128
    outer_size = length // inner_size
    leading = real_part.shape[:-1]
    real_in = real_part.reshape(leading + (outer_size, inner_size))
    imag_in = imag_part.reshape(leading + (outer_size, inner_size))
    highest = lax.Precision.HIGHEST
    outer_cos, outer_sin = angle_table(outer_size, outer_size, outer_size)
    real_mid = jnp.einsum("...pq,pk->...kq", real_in, outer_cos, precision=highest) + jnp.einsum(
        "...pq,pk->...kq", imag_in, outer_sin, precision=highest
    )
    imag_mid = jnp.einsum("...pq,pk->...kq", imag_in, outer_cos, precision=highest) - jnp.einsum(
        "...pq,pk->...kq", real_in, outer_sin, precision=highest
    )
    twist_cos, twist_sin = angle_table(outer_size, inner_size, length)
    real_twist = real_mid * twist_cos + imag_mid * twist_sin
    imag_twist = imag_mid * twist_cos - real_mid * twist_sin
    inner_cos, inner_sin = angle_table(inner_size, inner_size, inner_size)
    real_out = jnp.einsum("...kq,ql->...kl", real_twist, inner_cos, precision=highest) + jnp.einsum(
        "...kq,ql->...kl", imag_twist, inner_sin, precision=highest
    )
    imag_out = jnp.einsum("...kq,ql->...kl", imag_twist, inner_cos, precision=highest) - jnp.einsum(
        "...kq,ql->...kl", real_twist, inner_sin, precision=highest
    )
    real_out = jnp.swapaxes(real_out, -1, -2).reshape(leading + (length,))
    imag_out = jnp.swapaxes(imag_out, -1, -2).reshape(leading + (length,))
    return (real_out, imag_out)


def body(noise, elevation_library, tile_choice_index, family_heading_index, family_extent_index):
    line_count = noise.shape[1]
    side_cells = noise.shape[2]
    first_line = lax.axis_index(("row", "col")) * line_count
    v_index = first_line + lax.broadcasted_iota(jnp.int32, (line_count, side_cells), 0)
    u_index = lax.broadcasted_iota(jnp.int32, (line_count, side_cells), 1)
    amplitudes = amplitude(u_index, v_index, side_cells)
    real_part, imag_part = transform_last(noise[0] * amplitudes, noise[1] * amplitudes)
    spectrum = jnp.stack([real_part, imag_part])
    transposed = lax.all_to_all(
        spectrum.astype(jnp.bfloat16), ("row", "col"), split_axis=2, concat_axis=1, tiled=True
    ).astype(spectrum.dtype)
    turned = jnp.swapaxes(transposed, 1, 2)
    field_re, field_im = transform_last(turned[0], turned[1])
    fields = lax.all_to_all(
        jnp.stack([field_re, field_im]).astype(jnp.bfloat16),
        "col",
        split_axis=2,
        concat_axis=1,
        tiled=True,
    ).astype(jnp.float32)
    window_rows = fields.shape[1]
    window_columns = fields.shape[2]
    elevation_tiles = jnp.take(elevation_library, tile_choice_index, axis=0)
    slope_tangents = elevation_tiles.transpose(0, 2, 1, 3).reshape(window_rows, window_columns)
    secant = jnp.sqrt(1.0 + slope_tangents * slope_tangents)
    cohesion = 0.5 * jnp.exp(0.4 * fields[0])
    friction = 0.6 * jnp.exp(0.25 * fields[1])
    column_terms = jnp.stack(
        [cohesion * secant, friction / secant, slope_tangents / secant]
    ).astype(jnp.bfloat16)
    padded = extended(column_terms, (("row", 1), ("col", 2)), R)
    tile_width = min(128, window_columns)
    tile_count = window_columns // tile_width
    strip_span = tile_width + 2 * R
    strips = jnp.stack(
        [
            padded[:, :, tile_index * tile_width : tile_index * tile_width + strip_span]
            for tile_index in range(tile_count)
        ],
        axis=2,
    )
    kernel_width = 2 * R + 1
    shift_index = lax.broadcasted_iota(jnp.int32, (kernel_width, strip_span, tile_width), 0)
    strip_index = lax.broadcasted_iota(jnp.int32, (kernel_width, strip_span, tile_width), 1)
    out_index = lax.broadcasted_iota(jnp.int32, (kernel_width, strip_span, tile_width), 2)
    column_gap = strip_index - out_index
    offset_u = (shift_index - R).astype(jnp.float32)
    offset_v = (column_gap - R).astype(jnp.float32)
    inside_band = (column_gap >= 0) & (column_gap <= 2 * R)
    height, base_share = ellipsoid(
        offset_u[None],
        offset_v[None],
        family_heading_index[:, None, None, None],
        family_extent_index[:, None, None, None],
    )
    band_height = jnp.where(inside_band[None], height, 0.0).astype(jnp.bfloat16)
    band_share = jnp.where(inside_band[None], base_share, 0.0).astype(jnp.bfloat16)
    shifted = jnp.stack(
        [strips[:, row_shift : row_shift + window_rows] for row_shift in range(kernel_width)],
        axis=1,
    )
    resist_kernel = jnp.stack([band_share, band_height])
    resisting = jnp.einsum(
        "csxti,cfsio->fxto", shifted[0:2], resist_kernel, preferred_element_type=jnp.float32
    )
    driving = jnp.einsum(
        "sxti,fsio->fxto", shifted[2], band_height, preferred_element_type=jnp.float32
    )
    safety = resisting / driving
    family_low = jnp.min(safety, axis=0).reshape(window_rows, window_columns)
    half_width = window_columns // 2
    side_index = lax.axis_index("orient")
    own_half = lax.dynamic_slice_in_dim(family_low, side_index * half_width, half_width, 1)
    other_half = lax.dynamic_slice_in_dim(family_low, (1 - side_index) * half_width, half_width, 1)
    partner_half = partner(other_half, "orient", 0)
    return jnp.minimum(own_half, partner_half)


def solution(mesh):
    placed = (P(None, ("row", "col"), None), P(), P("row", "col"), P("orient"), P("orient"))
    return jax.shard_map(
        body, mesh=mesh, in_specs=placed, out_specs=P("row", ("col", "orient")), check_vma=False
    )
```

profile of v0, /device:TPU:0, one launch (start us, length us, event | category | flops | bytes accessed | tf_op | source)
XLA Modules:
  0.0 706.0 jit_solution(4212948183642729390)
XLA Ops:
  27.4 6.4 fusion.42
  33.8 7.0 fusion.40
  40.8 6.5 fusion.60
  48.7 6.8 fusion.61
  57.0 25.5 %copy.105 = bf16[2,256,4096]{1,0,2:T(2,128)(2,1)S(1)} copy(bf16[2,256,4096]{1,2,0:T(8,128)(2,1)S(1)} %pad_maximum_fusion.2) | data formatting | bytes 8388608 | tf_op jit(solution)/shard_map/stack | solution.py:108
  82.5 99.9 %all_to_all.27 = bf16[2,256,4096]{1,0,2:T(2,128)(2,1)S(1)} all-to-all(bf16[2,256,4096]{1,0,2:T(2,128)(2,1)S(1)} %copy.105), channel_id=1, replica_groups=mesh['row'=2,'col'=8,'orient'=2] {'row','col'}, dimensions={2} | all-to-all | bytes 8388608 | tf_op jit(solution)/shard_map/all_to_all | solution.py:109
  216.7 6.8 fusion.34
  223.5 6.8 fusion.32
  230.3 7.2 %fusion.62 = bf16[256,128,32]{0,1,2:T(8,128)(2,1)S(1)} fusion(f32[256,32,128]{0,2,1:T(8,128)S(1)} %fusion.34, f32[256,32,128]{2,1,0:T(8,128)S(1)} %get-tuple-element.5), kind=kOutput, calls=%fused_computation.116 | convolution fusion | flops 1612939264 | bytes 10485760 | tf_op jit(solution)/shard_map/...kq,ql->...kl/dot_general | solution.py:89
  238.7 6.7 fusion.63
  247.0 27.2 %copy.116 = bf16[2,256,4096]{1,0,2:T(2,128)(2,1)} copy(bf16[2,256,4096]{1,2,0:T(8,128)(2,1)S(1)} %pad_maximum_fusion.3) | data formatting | bytes 8388608 | tf_op jit(solution)/shard_map/stack | solution.py:115
  298.7 74.4 %all-to-all-done.1 = bf16[2,256,4096]{1,0,2:T(2,128)(2,1)} async-done(((bf16[2,256,4096]{1,0,2:T(2,128)(2,1)}), bf16[2,256,4096]{1,0,2:T(2,128)(2,1)}, u32[]{:S(2)}, u32[]{:S(2)}) %all-to-all-start.1) | async-done | bytes 4194336 | tf_op jit(solution)/shard_map/all_to_all | solution.py:114
  412.2 12.7 %concatenate.10 = bf16[3,2064,512]{1,2,0:T(8,128)(2,1)} concatenate(bf16[3,8,512]{1,2,0:T(8,128)(2,1)} %copy-done.11, bf16[3,2048,512]{1,2,0:T(8,128)(2,1)} %copy-done.2, bf16[3,8,512]{1,2,0:T(8,128)(2,1)} %collective-permute-done.1), dimensions={1} | concatenate | bytes 12681216 | tf_op jit(solution)/shard_map/concatenate | solution.py:21
  444.1 6.7 fusion.18
  450.9 6.7 fusion.17
  457.6 6.7 fusion.16
  464.2 6.9 fusion.15
  471.1 6.7 fusion.14
  477.8 6.7 fusion.13
  484.5 6.9 fusion.12
  491.4 6.7 fusion.11
  498.1 6.7 fusion.10
  504.8 7.0 fusion.9
  511.9 6.7 fusion.8
  518.6 6.6 fusion.7
  525.2 6.8 fusion.6
  532.1 6.7 fusion.5
  538.8 6.7 fusion.4
  545.5 6.6 fusion.3
  552.2 51.8 %fusion = f32[4,128,2048,4,1,1]{2,1,5,4,3,0:T(8,128)} fusion(bf16[3,17,2048,4,144]{2,4,1,0,3:T(8,128)(2,1)} %fusion.3, bf16[2,4,17,144,128,1]{4,3,2,0,5,1:T(8,128)(2,1)} %maximum_bitcast_fusion.4), kind=kOutput, calls=%fused_computation.2 | convolution fusion | flops 41070624768 | bytes 102006784 | tf_op jit(solution)/shard_map/csxti,cfsio->fxto/dot_general | solution.py:163
  604.1 42.4 %fusion.2 = f32[128,2048,4]{1,0,2:T(8,128)} fusion(f32[4,128,2048,4,1,1]{2,1,5,4,3,0:T(8,128)} %fusion, bf16[3,17,2048,4,144]{2,4,1,0,3:T(8,128)(2,1)} %fusion.3, f32[4]{0:T(128)S(1)} %copy-done.16, f32[4]{0:T(128)S(1)} %copy-done.14, f32[4]{0:T(128)S(1)} %copy-done.20, f32[17,144,128]{2,1,0:T(8,128)S(1)} %copy-done.8, f32[4]{0:T(128)S(1)} %copy-done.22, ...), kind=kOutput, calls=%fused_computation.6 | convolution fusion | flops 20562706432 | bytes 62646420 | tf_op jit(solution)/shard_map/sxti,fsio->fxto/dot_general | solution.py:166
  656.6 45.4 %collective-permute-done.4 = f32[2048,256]{1,0:T(8,128)} collective-permute-done((f32[2048,256]{1,0:T(8,128)}, f32[2048,256]{1,0:T(8,128)}, u32[]{:S(2)}, u32[]{:S(2)}) %collective-permute-start.4) | collective-permute-done | bytes 2097184 | tf_op jit(solution)/shard_map/ppermute | solution.py:33
  (121 shorter events, 163.6 us)
Async XLA Ops:
  0.0 279.3 %copy-start = (f32[16,128,128]{2,1,0:T(8,128)S(1)}, f32[16,128,128]{2,1,0:T(8,128)}, u32[]{:S(2)}) copy-start(f32[16,128,128]{2,1,0:T(8,128)} %param.6) | copy-start | bytes 3145732
  207.9 3.8 copy-start.3
  207.9 3.8 copy-start.4
  274.2 4.9 copy-start.12
  274.2 98.9 %all-to-all-start.1 = ((bf16[2,256,4096]{1,0,2:T(2,128)(2,1)}), bf16[2,256,4096]{1,0,2:T(2,128)(2,1)}, u32[]{:S(2)}, u32[]{:S(2)}) async-start(bf16[2,256,4096]{1,0,2:T(2,128)(2,1)} %copy.116), calls=%async_computation.1 | async-start | bytes 8388608 | tf_op jit(solution)/shard_map/all_to_all | solution.py:114
  292.2 6.3 copy-start.25
  292.2 6.3 copy-start.26
  297.2 103.9 %copy-start.23 = (f32[17]{0:T(128)}, f32[17]{0:T(128)S(1)}, u32[]{:S(2)}) copy-start(f32[17]{0:T(128)S(1)} %add_convert_fusion.3) | copy-start | bytes 208
  297.3 103.8 %copy-start.9 = (pred[17,144,128]{2,1,0:T(8,128)(4,1)}, pred[17,144,128]{2,1,0:T(8,128)(4,1)S(1)}, u32[]{:S(2)}) copy-start(pred[17,144,128]{2,1,0:T(8,128)(4,1)S(1)} %fusion.76) | copy-start | bytes 940036
  298.6 102.5 %copy-start.13 = (f32[4]{0:T(128)}, f32[4]{0:T(128)S(1)}, u32[]{:S(2)}) copy-start(f32[4]{0:T(128)S(1)} %get-tuple-element.34) | copy-start | bytes 52
  298.6 102.5 %copy-start.15 = (f32[4]{0:T(128)}, f32[4]{0:T(128)S(1)}, u32[]{:S(2)}) copy-start(f32[4]{0:T(128)S(1)} %get-tuple-element.35) | copy-start | bytes 52
  298.6 102.5 %copy-start.17 = (f32[4]{0:T(128)}, f32[4]{0:T(128)S(1)}, u32[]{:S(2)}) copy-start(f32[4]{0:T(128)S(1)} %get-tuple-element.36) | copy-start | bytes 52
  298.6 102.5 %copy-start.19 = (f32[4]{0:T(128)}, f32[4]{0:T(128)S(1)}, u32[]{:S(2)}) copy-start(f32[4]{0:T(128)S(1)} %get-tuple-element.39) | copy-start | bytes 52
  298.6 102.5 %copy-start.21 = (f32[4]{0:T(128)}, f32[4]{0:T(128)S(1)}, u32[]{:S(2)}) copy-start(f32[4]{0:T(128)S(1)} %get-tuple-element.40) | copy-start | bytes 52
  380.0 2.2 copy-start.6
  382.2 2.2 copy-start.5
  389.7 11.5 %copy-start.7 = (f32[17,144,128]{2,1,0:T(8,128)S(1)}, f32[17,144,128]{2,1,0:T(8,128)}, u32[]{:S(2)}) copy-start(f32[17,144,128]{2,1,0:T(8,128)} %add_convert_fusion.2) | copy-start | bytes 3760132
  393.5 2.7 copy-start.2
  396.4 11.5 %collective-permute-start = (bf16[3,8,512]{1,2,0:T(8,128)(2,1)S(1)}, bf16[3,8,512]{1,2,0:T(8,128)(2,1)S(1)}, u32[]{:S(2)}, u32[]{:S(2)}) collective-permute-start(bf16[3,8,512]{1,2,0:T(8,128)(2,1)S(1)} %get-tuple-element.20), channel_id=1, source_target_pairs={{0,16},{1,17},{2,18},{3,19},{4,20},{5,21},{6,22},{7,23},{8,24},{9,... | collective-permute-start | bytes 73736 | tf_op jit(solution)/shard_map/ppermute | solution.py:23
  399.8 12.4 %collective-permute-start.1 = (bf16[3,8,512]{1,2,0:T(8,128)(2,1)S(1)}, bf16[3,8,512]{1,2,0:T(8,128)(2,1)}, u32[]{:S(2)}, u32[]{:S(2)}) collective-permute-start(bf16[3,8,512]{1,2,0:T(8,128)(2,1)S(1)} %get-tuple-element.19), channel_id=1, source_target_pairs={{16,0},{17,1},{18,2},{19,3},{20,4},{21,5},{22,6},{23,7},{24,8},{25... | collective-permute-start | bytes 73736 | tf_op jit(solution)/shard_map/ppermute | solution.py:25
  425.9 7.0 collective-permute-start.2
  427.2 5.7 collective-permute-start.3
  552.2 51.9 %copy-start.8 = (f32[17,144,128]{2,1,0:T(8,128)S(1)}, f32[17,144,128]{2,1,0:T(8,128)}, u32[]{:S(2)}) copy-start(f32[17,144,128]{2,1,0:T(8,128)} %add_convert_fusion.2) | copy-start | bytes 3760132
  552.2 51.9 %copy-start.10 = (pred[17,144,128]{2,1,0:T(8,128)(4,1)S(1)}, pred[17,144,128]{2,1,0:T(8,128)(4,1)}, u32[]{:S(2)}) copy-start(pred[17,144,128]{2,1,0:T(8,128)(4,1)} %copy-done.9) | copy-start | bytes 940036
  552.2 51.9 %copy-start.14 = (f32[4]{0:T(128)S(1)}, f32[4]{0:T(128)}, u32[]{:S(2)}) copy-start(f32[4]{0:T(128)} %copy-done.13) | copy-start | bytes 52
  552.2 51.9 %copy-start.16 = (f32[4]{0:T(128)S(1)}, f32[4]{0:T(128)}, u32[]{:S(2)}) copy-start(f32[4]{0:T(128)} %copy-done.15) | copy-start | bytes 52
  552.2 51.9 %copy-start.18 = (f32[4]{0:T(128)S(1)}, f32[4]{0:T(128)}, u32[]{:S(2)}) copy-start(f32[4]{0:T(128)} %copy-done.17) | copy-start | bytes 52
  552.2 51.9 %copy-start.20 = (f32[4]{0:T(128)S(1)}, f32[4]{0:T(128)}, u32[]{:S(2)}) copy-start(f32[4]{0:T(128)} %copy-done.19) | copy-start | bytes 52
  552.2 51.9 %copy-start.22 = (f32[4]{0:T(128)S(1)}, f32[4]{0:T(128)}, u32[]{:S(2)}) copy-start(f32[4]{0:T(128)} %copy-done.21) | copy-start | bytes 52
  552.2 51.9 %copy-start.24 = (f32[17]{0:T(128)S(1)}, f32[17]{0:T(128)}, u32[]{:S(2)}) copy-start(f32[17]{0:T(128)} %copy-done.23) | copy-start | bytes 208
  653.3 48.7 %collective-permute-start.4 = (f32[2048,256]{1,0:T(8,128)}, f32[2048,256]{1,0:T(8,128)}, u32[]{:S(2)}, u32[]{:S(2)}) collective-permute-start(f32[2048,256]{1,0:T(8,128)} %copy.147), channel_id=1, source_target_pairs={{0,1},{1,0},{2,3},{3,2},{4,5},{5,4},{6,7},{7,6},{8,9},{9,8},{10,11... | collective-permute-start | bytes 6291464 | tf_op jit(solution)/shard_map/ppermute | solution.py:33
  654.8 51.0 %copy-start.1 = (f32[16,128,128]{2,1,0:T(8,128)S(1)}, f32[16,128,128]{2,1,0:T(8,128)}, u32[]{:S(2)}) copy-start(f32[16,128,128]{2,1,0:T(8,128)} %param.6) | copy-start | bytes 3145732
  (1 other events, 0.7 us)
where the time goes:
time: 711 us; the launch traced here: 706 us
  local copies, waits for them, and re-layouts  243 us (34%)
  matrix products  178 us (25%)
  waiting for transfers between devices  125 us (18%)
  blocking collectives  99.9 us (14%)
  other arithmetic  45.5 us (6%)
  starting transfers between devices  13.6 us (2%)
    unnamed x75, local copies, waits for them, and re-layouts  122 us
    all_to_all x1, blocking collectives, body(): lax.all_to_all(spectrum.astype(jnp.bfloat16), ('row', 'col'), split_axis=...  99.9 us
    all_to_all x1, waiting for transfers between devices, body(): lax.all_to_all(jnp.stack([field_re, field_im]).astype(jnp.bfloat16), 'col...  74.4 us
    dot_general x1, matrix products, body(): jnp.einsum('csxti,cfsio->fxto', shifted[0:2], resist_kernel, preferred_el...  51.8 us
    ppermute x1, waiting for transfers between devices, partner(): lax.ppermute(x, axis, [(i, i ^ 1 << bit) for i in range(lax.axis_size(axi...  45.4 us
    dot_general x1, matrix products, body(): jnp.einsum('sxti,fsio->fxto', shifted[2], band_height, preferred_element_...  42.4 us
    another operation x1, local copies, waits for them, and re-layouts, body(): jnp.stack([field_re, field_im]).astype(jnp.bfloat16)  27.2 us
    another operation x1, local copies, waits for them, and re-layouts, body(): spectrum = jnp.stack([real_part, imag_part])  25.5 us
  transfers between devices with their start and end apart: 6, of which 4 were waited for; matrix products, arithmetic and copies ran while one was open for 4% of the time, Pallas kernels for 0%

commit v1 on v0

--- a/solution.py
+++ b/solution.py
@@ -10,6 +10,29 @@
 nugget_share = 0.3
 peak_share = 1024.0 / (2.0 * math.pi)
 cutoff_ratio = 32.0
+
+
+def split_up(value, dim, size):
+    shape = value.shape
+    pieces = value.reshape(*shape[:dim], size, shape[dim] // size, *shape[dim + 1 :])
+    return jnp.moveaxis(pieces, dim, 0)
+
+
+def laid_out(blocks, dim):
+    dims = list(blocks.shape[1:])
+    dims[dim] *= blocks.shape[0]
+    return jnp.moveaxis(blocks, 0, dim).reshape(dims)
+
+
+def exchange_directly(shard, axis, split_dim, concat_dim):
+    length, here = (lax.axis_size(axis), lax.axis_index(axis))
+    blocks = split_up(shard, split_dim, length)
+    outs = [blocks[here]]
+    for turn in range(1, length):
+        sent = blocks[(here + turn) % length]
+        outs.append(lax.ppermute(sent, axis, [(i, (i + turn) % length) for i in range(length)]))
+    blocks = jnp.stack(outs)[(here - jnp.arange(length)) % length]
+    return laid_out(blocks, concat_dim)
 
 
 def extended(cells, sides, width):
@@ -111,12 +134,8 @@
     ).astype(spectrum.dtype)
     turned = jnp.swapaxes(transposed, 1, 2)
     field_re, field_im = transform_last(turned[0], turned[1])
-    fields = lax.all_to_all(
-        jnp.stack([field_re, field_im]).astype(jnp.bfloat16),
-        "col",
-        split_axis=2,
-        concat_axis=1,
-        tiled=True,
+    fields = exchange_directly(
+        jnp.stack([field_re, field_im]).astype(jnp.bfloat16), "col", 2, 1
     ).astype(jnp.float32)
     window_rows = fields.shape[1]
     window_columns = fields.shape[2]

time: 711 us -> 698 us (0.982)
  the two profiles are of different devices: /device:TPU:0 before, /device:TPU:24 now
where the time goes in v1:
time: 698 us; the launch traced here: 693 us
  local copies, waits for them, and re-layouts  251 us (36%)
  matrix products  178 us (26%)
  waiting for transfers between devices  170 us (24%)
  other arithmetic  52.9 us (8%)
  starting transfers between devices  39.6 us (6%)
    unnamed x82, local copies, waits for them, and re-layouts  130 us
    all_to_all x1, waiting for transfers between devices, body(): lax.all_to_all(spectrum.astype(jnp.bfloat16), ('row', 'col'), split_axis=...  67 us
    ppermute x7, waiting for transfers between devices, exchange_directly(): lax.ppermute(sent, axis, [(i, (i + turn) % length) for i in range(length)])  57.1 us
    dot_general x1, matrix products, body(): jnp.einsum('csxti,cfsio->fxto', shifted[0:2], resist_kernel, preferred_el...  52 us
    ppermute x1, waiting for transfers between devices, partner(): lax.ppermute(x, axis, [(i, i ^ 1 << bit) for i in range(lax.axis_size(axi...  43.9 us
    dot_general x1, matrix products, body(): jnp.einsum('sxti,fsio->fxto', shifted[2], band_height, preferred_element_...  42.4 us
    another operation x1, local copies, waits for them, and re-layouts, body(): spectrum = jnp.stack([real_part, imag_part])  27.5 us
    ppermute x7, starting transfers between devices, exchange_directly(): lax.ppermute(sent, axis, [(i, (i + turn) % length) for i in range(length)])  22.8 us
  transfers between devices with their start and end apart: 13, of which 5 were waited for; matrix products, arithmetic and copies ran while one was open for 8% of the time, Pallas kernels for 0%

profile of v1, /device:TPU:24, one launch (start us, length us, event | category | flops | bytes accessed | tf_op | source)
XLA Modules:
  0.0 692.9 jit_solution(16844883480790538151)
XLA Ops:
  33.5 6.8 fusion.38
  48.2 6.5 fusion.59
  56.3 27.5 %copy.121 = bf16[2,256,4096]{1,0,2:T(2,128)(2,1)} copy(bf16[2,256,4096]{1,2,0:T(8,128)(2,1)S(1)} %pad_maximum_fusion.2) | data formatting | bytes 8388608 | tf_op jit(solution)/shard_map/stack | solution.py:131
  110.0 67.0 %all-to-all-done = bf16[2,256,4096]{1,0,2:T(2,128)(2,1)} async-done(((bf16[2,256,4096]{1,0,2:T(2,128)(2,1)}), bf16[2,256,4096]{1,0,2:T(2,128)(2,1)}, u32[]{:S(2)}, u32[]{:S(2)}) %all-to-all-start) | async-done | bytes 4194336 | tf_op jit(solution)/shard_map/all_to_all | solution.py:132
  213.5 7.0 %fusion.30 = f32[256,32,128]{0,2,1:T(8,128)S(1)} fusion(f32[256,32,128]{2,1,0:T(8,128)S(1)} %get-tuple-element.6), kind=kOutput, calls=%fused_computation.97 | convolution fusion | flops 1610842112 | bytes 8388608 | tf_op jit(solution)/shard_map/...kq,ql->...kl/dot_general | solution.py:115
  220.5 6.6 fusion.32
  227.1 7.2 %fusion.61 = bf16[256,128,32]{0,1,2:T(8,128)(2,1)S(1)} fusion(f32[256,32,128]{0,2,1:T(8,128)S(1)} %fusion.30, f32[256,32,128]{2,1,0:T(8,128)S(1)} %get-tuple-element.5), kind=kOutput, calls=%fused_computation.131 | convolution fusion | flops 1612939264 | bytes 10485760 | tf_op jit(solution)/shard_map/...kq,ql->...kl/dot_general | solution.py:115
  235.5 6.8 fusion.60
  272.7 12.6 %collective-permute-start.6 = (bf16[2,256,512]{2,1,0:T(8,128)(2,1)S(1)}, bf16[2,256,512]{2,1,0:T(8,128)(2,1)S(1)}, u32[]{:S(2)}, u32[]{:S(2)}) collective-permute-start(bf16[2,256,512]{2,1,0:T(8,128)(2,1)S(1)} %bitcast.282), channel_id=1, source_target_pairs={{0,14},{2,0},{4,2},{6,4},{8,6},{10,8},{12,10},{14,12},{1,15},{3,1}... | collective-permute-start | bytes 1572872 | tf_op jit(solution)/shard_map/ppermute | solution.py:33
  287.2 43.5 %collective-permute-done.2 = bf16[2,256,512]{2,1,0:T(8,128)(2,1)} collective-permute-done((bf16[2,256,512]{2,1,0:T(8,128)(2,1)}, bf16[2,256,512]{2,1,0:T(8,128)(2,1)}, u32[]{:S(2)}, u32[]{:S(2)}) %collective-permute-start.2) | collective-permute-done | bytes 524320 | tf_op jit(solution)/shard_map/ppermute | solution.py:33
  332.6 13.5 %collective-permute-done.3 = bf16[2,256,512]{2,1,0:T(8,128)(2,1)} collective-permute-done((bf16[2,256,512]{2,1,0:T(8,128)(2,1)}, bf16[2,256,512]{2,1,0:T(8,128)(2,1)}, u32[]{:S(2)}, u32[]{:S(2)}) %collective-permute-start.3) | collective-permute-done | bytes 524320 | tf_op jit(solution)/shard_map/ppermute | solution.py:33
  374.4 7.1 %multiply_convert_fusion.2 = (bf16[1,2048,512]{1,2,0:T(8,128)(2,1)S(1)}, bf16[1,2048,512]{1,2,0:T(8,128)(2,1)S(1)}, bf16[1,2048,512]{1,2,0:T(8,128)(2,1)S(1)}) fusion(f32[1,2048,512]{1,2,0:T(8,128)} %copy.168, f32[1,2048,512]{1,2,0:T(8,128)} %reshape.273, f32[1,2048,512]{1,2,0:T(8,128)} %copy.169), kind=kLoop, calls=%fused_computation.84 | loop fusion | flops 8388608 | bytes 18874368 | tf_op jit(solution)/shard_map/convert.1
  398.8 12.7 %concatenate.12 = bf16[3,2064,512]{1,2,0:T(8,128)(2,1)} concatenate(bf16[3,8,512]{1,2,0:T(8,128)(2,1)} %copy-done.11, bf16[3,2048,512]{1,2,0:T(8,128)(2,1)} %copy-done.2, bf16[3,8,512]{1,2,0:T(8,128)(2,1)} %collective-permute-done.8), dimensions={1} | concatenate | bytes 12681216 | tf_op jit(solution)/shard_map/concatenate | solution.py:44
  432.5 6.7 fusion.18
  439.2 6.7 fusion.17
  445.9 6.7 fusion.16
  452.6 6.8 fusion.15
  459.4 6.7 fusion.14
  466.1 6.7 fusion.13
  472.8 6.9 fusion.12
  479.7 6.7 fusion.11
  486.3 6.7 fusion.10
  493.0 7.0 %fusion.9 = bf16[3,17,2048,4,144]{2,4,1,0,3:T(8,128)(2,1)} fusion(bf16[3,17,2048,4,144]{2,4,1,0,3:T(8,128)(2,1)} %fusion.10, bf16[3,2064,4,144]{1,3,0,2:T(8,128)(2,1)S(1)} %pad_maximum_fusion), kind=kLoop, calls=%fused_computation.39 | loop fusion | bytes 14155776
  500.1 6.7 fusion.8
  506.8 6.7 fusion.7
  513.5 6.9 fusion.6
  520.4 6.7 fusion.5
  527.1 6.7 fusion.4
  533.7 6.7 fusion.3
  540.5 52.0 %fusion = f32[4,128,2048,4,1,1]{2,1,5,4,3,0:T(8,128)} fusion(bf16[3,17,2048,4,144]{2,4,1,0,3:T(8,128)(2,1)} %fusion.3, bf16[2,4,17,144,128,1]{4,3,2,0,5,1:T(8,128)(2,1)} %maximum_bitcast_fusion.4), kind=kOutput, calls=%fused_computation.3 | convolution fusion | flops 41070624768 | bytes 102006784 | tf_op jit(solution)/shard_map/csxti,cfsio->fxto/dot_general | solution.py:182
  592.5 42.4 %fusion.2 = f32[128,2048,4]{1,0,2:T(8,128)} fusion(f32[4,128,2048,4,1,1]{2,1,5,4,3,0:T(8,128)} %fusion, bf16[3,17,2048,4,144]{2,4,1,0,3:T(8,128)(2,1)} %fusion.3, f32[4]{0:T(128)S(1)} %copy-done.16, f32[4]{0:T(128)S(1)} %copy-done.14, f32[4]{0:T(128)S(1)} %copy-done.20, f32[17,144,128]{2,1,0:T(8,128)S(1)} %copy-done.7, f32[4]{0:T(128)S(1)} %copy-done.22, ...), kind=kOutput, calls=%fused_computation.7 | convolution fusion | flops 20562706432 | bytes 62646420 | tf_op jit(solution)/shard_map/sxti,fsio->fxto/dot_general | solution.py:185
  645.0 43.9 %collective-permute-done.11 = f32[2048,256]{1,0:T(8,128)} collective-permute-done((f32[2048,256]{1,0:T(8,128)}, f32[2048,256]{1,0:T(8,128)}, u32[]{:S(2)}, u32[]{:S(2)}) %collective-permute-start.11) | collective-permute-done | bytes 2097184 | tf_op jit(solution)/shard_map/ppermute | solution.py:56
  (152 shorter events, 221.2 us)
Async XLA Ops:
  0.0 90.2 %copy-start = (f32[16,128,128]{2,1,0:T(8,128)S(1)}, f32[16,128,128]{2,1,0:T(8,128)}, u32[]{:S(2)}) copy-start(f32[16,128,128]{2,1,0:T(8,128)} %param.6) | copy-start | bytes 3145732
  83.8 93.2 %all-to-all-start = ((bf16[2,256,4096]{1,0,2:T(2,128)(2,1)}), bf16[2,256,4096]{1,0,2:T(2,128)(2,1)}, u32[]{:S(2)}, u32[]{:S(2)}) async-start(bf16[2,256,4096]{1,0,2:T(2,128)(2,1)} %copy.121), calls=%async_computation | async-start | bytes 8388608 | tf_op jit(solution)/shard_map/all_to_all | solution.py:132
  248.3 22.2 %collective-permute-start = (bf16[2,256,512]{2,1,0:T(8,128)(2,1)}, bf16[2,256,512]{2,1,0:T(8,128)(2,1)}, u32[]{:S(2)}, u32[]{:S(2)}) collective-permute-start(bf16[2,256,512]{2,1,0:T(8,128)(2,1)} %bitcast.283), channel_id=1, source_target_pairs={{0,2},{2,4},{4,6},{6,8},{8,10},{10,12},{12,14},{14,0},{1,3},{3,5},... | collective-permute-start | bytes 1572872 | tf_op jit(solution)/shard_map/ppermute | solution.py:33
  251.7 20.9 %collective-permute-start.1 = (bf16[2,256,512]{2,1,0:T(8,128)(2,1)}, bf16[2,256,512]{2,1,0:T(8,128)(2,1)}, u32[]{:S(2)}, u32[]{:S(2)}) collective-permute-start(bf16[2,256,512]{2,1,0:T(8,128)(2,1)} %bitcast.281), channel_id=1, source_target_pairs={{0,4},{2,6},{4,8},{6,10},{8,12},{10,14},{12,0},{14,2},{1,5},{3,7},... | collective-permute-start | bytes 1572872 | tf_op jit(solution)/shard_map/ppermute | solution.py:33
  255.7 14.3 %copy-start.8 = (bf16[2,256,1,512]{1,3,2,0:T(8,128)(2,1)S(1)}, bf16[2,256,1,512]{1,3,2,0:T(8,128)(2,1)}, u32[]{:S(2)}) copy-start(bf16[2,256,1,512]{1,3,2,0:T(8,128)(2,1)} %get-tuple-element.32) | copy-start | bytes 1572868
  257.0 91.0 %collective-permute-start.4 = (bf16[2,256,512]{2,1,0:T(8,128)(2,1)S(1)}, bf16[2,256,512]{2,1,0:T(8,128)(2,1)S(1)}, u32[]{:S(2)}, u32[]{:S(2)}) collective-permute-start(bf16[2,256,512]{2,1,0:T(8,128)(2,1)S(1)} %bitcast.280), channel_id=1, source_target_pairs={{0,10},{2,12},{4,14},{6,0},{8,2},{10,4},{12,6},{14,8},{1,11},{3,13... | collective-permute-start | bytes 1572872 | tf_op jit(solution)/shard_map/ppermute | solution.py:33
  264.9 65.8 %collective-permute-start.2 = (bf16[2,256,512]{2,1,0:T(8,128)(2,1)}, bf16[2,256,512]{2,1,0:T(8,128)(2,1)}, u32[]{:S(2)}, u32[]{:S(2)}) collective-permute-start(bf16[2,256,512]{2,1,0:T(8,128)(2,1)} %bitcast.285), channel_id=1, source_target_pairs={{0,6},{2,8},{4,10},{6,12},{8,14},{10,0},{12,2},{14,4},{1,7},{3,9},... | collective-permute-start | bytes 1572872 | tf_op jit(solution)/shard_map/ppermute | solution.py:33
  268.0 78.1 %collective-permute-start.3 = (bf16[2,256,512]{2,1,0:T(8,128)(2,1)}, bf16[2,256,512]{2,1,0:T(8,128)(2,1)}, u32[]{:S(2)}, u32[]{:S(2)}) collective-permute-start(bf16[2,256,512]{2,1,0:T(8,128)(2,1)} %bitcast.32), channel_id=1, source_target_pairs={{0,8},{2,10},{4,12},{6,14},{8,0},{10,2},{12,4},{14,6},{1,9},{3,11}... | collective-permute-start | bytes 1572872 | tf_op jit(solution)/shard_map/ppermute | solution.py:33
  270.5 78.3 %collective-permute-start.5 = (bf16[2,256,512]{2,1,0:T(8,128)(2,1)S(1)}, bf16[2,256,512]{2,1,0:T(8,128)(2,1)S(1)}, u32[]{:S(2)}, u32[]{:S(2)}) collective-permute-start(bf16[2,256,512]{2,1,0:T(8,128)(2,1)S(1)} %bitcast.284), channel_id=1, source_target_pairs={{0,12},{2,14},{4,0},{6,2},{8,4},{10,6},{12,8},{14,10},{1,13},{3,15... | collective-permute-start | bytes 1572872 | tf_op jit(solution)/shard_map/ppermute | solution.py:33
  272.7 77.0 %collective-permute-start.6 = (bf16[2,256,512]{2,1,0:T(8,128)(2,1)S(1)}, bf16[2,256,512]{2,1,0:T(8,128)(2,1)S(1)}, u32[]{:S(2)}, u32[]{:S(2)}) collective-permute-start(bf16[2,256,512]{2,1,0:T(8,128)(2,1)S(1)} %bitcast.282), channel_id=1, source_target_pairs={{0,14},{2,0},{4,2},{6,4},{8,6},{10,8},{12,10},{14,12},{1,15},{3,1}... | collective-permute-start | bytes 1572872 | tf_op jit(solution)/shard_map/ppermute | solution.py:33
  381.6 8.8 %copy-start.6 = (f32[17,144,128]{2,1,0:T(8,128)S(1)}, f32[17,144,128]{2,1,0:T(8,128)}, u32[]{:S(2)}) copy-start(f32[17,144,128]{2,1,0:T(8,128)} %add_convert_fusion.2) | copy-start | bytes 3760132
  381.6 8.8 %copy-start.9 = (pred[17,144,128]{2,1,0:T(8,128)(4,1)S(1)}, pred[17,144,128]{2,1,0:T(8,128)(4,1)}, u32[]{:S(2)}) copy-start(pred[17,144,128]{2,1,0:T(8,128)(4,1)} %fusion.74) | copy-start | bytes 940036
  381.6 8.8 %copy-start.13 = (f32[4]{0:T(128)S(1)}, f32[4]{0:T(128)}, u32[]{:S(2)}) copy-start(f32[4]{0:T(128)} %get-tuple-element.42) | copy-start | bytes 52
  381.6 8.8 %copy-start.15 = (f32[4]{0:T(128)S(1)}, f32[4]{0:T(128)}, u32[]{:S(2)}) copy-start(f32[4]{0:T(128)} %get-tuple-element.43) | copy-start | bytes 52
  381.6 8.8 %copy-start.17 = (f32[4]{0:T(128)S(1)}, f32[4]{0:T(128)}, u32[]{:S(2)}) copy-start(f32[4]{0:T(128)} %get-tuple-element.44) | copy-start | bytes 52
  381.6 8.8 %copy-start.19 = (f32[4]{0:T(128)S(1)}, f32[4]{0:T(128)}, u32[]{:S(2)}) copy-start(f32[4]{0:T(128)} %get-tuple-element.47) | copy-start | bytes 52
  381.6 8.8 %copy-start.21 = (f32[4]{0:T(128)S(1)}, f32[4]{0:T(128)}, u32[]{:S(2)}) copy-start(f32[4]{0:T(128)} %get-tuple-element.48) | copy-start | bytes 52
  381.6 8.8 %copy-start.23 = (f32[17]{0:T(128)S(1)}, f32[17]{0:T(128)}, u32[]{:S(2)}) copy-start(f32[17]{0:T(128)} %add_convert_fusion.3) | copy-start | bytes 208
  385.5 10.5 %collective-permute-start.7 = (bf16[3,8,512]{1,2,0:T(8,128)(2,1)S(1)}, bf16[3,8,512]{1,2,0:T(8,128)(2,1)S(1)}, u32[]{:S(2)}, u32[]{:S(2)}) collective-permute-start(bf16[3,8,512]{1,2,0:T(8,128)(2,1)S(1)} %get-tuple-element.20), channel_id=1, source_target_pairs={{0,16},{1,17},{2,18},{3,19},{4,20},{5,21},{6,22},{7,23},{8,24},{9,... | collective-permute-start | bytes 73736 | tf_op jit(solution)/shard_map/ppermute | solution.py:46
  389.0 9.8 %collective-permute-start.8 = (bf16[3,8,512]{1,2,0:T(8,128)(2,1)S(1)}, bf16[3,8,512]{1,2,0:T(8,128)(2,1)}, u32[]{:S(2)}, u32[]{:S(2)}) collective-permute-start(bf16[3,8,512]{1,2,0:T(8,128)(2,1)S(1)} %get-tuple-element.19), channel_id=1, source_target_pairs={{16,0},{17,1},{18,2},{19,3},{20,4},{21,5},{22,6},{23,7},{24,8},{25... | collective-permute-start | bytes 73736 | tf_op jit(solution)/shard_map/ppermute | solution.py:48
  412.5 8.8 %collective-permute-start.10 = (bf16[3,2064,8]{1,2,0:T(8,128)(2,1)S(1)}, bf16[3,2064,8]{1,2,0:T(8,128)(2,1)S(1)}, u32[]{:S(2)}, u32[]{:S(2)}) collective-permute-start(bf16[3,2064,8]{1,2,0:T(8,128)(2,1)S(1)} %get-tuple-element.18), channel_id=1, source_target_pairs={{2,0},{4,2},{6,4},{8,6},{10,8},{12,10},{14,12},{3,1},{5,3},{7,5},{... | collective-permute-start | bytes 297224 | tf_op jit(solution)/shard_map/ppermute | solution.py:48
  414.4 6.8 collective-permute-start.9
  540.4 52.0 %copy-start.7 = (f32[17,144,128]{2,1,0:T(8,128)S(1)}, f32[17,144,128]{2,1,0:T(8,128)}, u32[]{:S(2)}) copy-start(f32[17,144,128]{2,1,0:T(8,128)} %add_convert_fusion.2) | copy-start | bytes 3760132
  540.4 52.0 %copy-start.10 = (pred[17,144,128]{2,1,0:T(8,128)(4,1)S(1)}, pred[17,144,128]{2,1,0:T(8,128)(4,1)}, u32[]{:S(2)}) copy-start(pred[17,144,128]{2,1,0:T(8,128)(4,1)} %fusion.74) | copy-start | bytes 940036
  540.4 52.0 %copy-start.14 = (f32[4]{0:T(128)S(1)}, f32[4]{0:T(128)}, u32[]{:S(2)}) copy-start(f32[4]{0:T(128)} %get-tuple-element.42) | copy-start | bytes 52
  540.4 52.0 %copy-start.16 = (f32[4]{0:T(128)S(1)}, f32[4]{0:T(128)}, u32[]{:S(2)}) copy-start(f32[4]{0:T(128)} %get-tuple-element.43) | copy-start | bytes 52
  540.4 52.0 %copy-start.18 = (f32[4]{0:T(128)S(1)}, f32[4]{0:T(128)}, u32[]{:S(2)}) copy-start(f32[4]{0:T(128)} %get-tuple-element.44) | copy-start | bytes 52
  540.4 52.0 %copy-start.20 = (f32[4]{0:T(128)S(1)}, f32[4]{0:T(128)}, u32[]{:S(2)}) copy-start(f32[4]{0:T(128)} %get-tuple-element.47) | copy-start | bytes 52
  540.4 52.0 %copy-start.22 = (f32[4]{0:T(128)S(1)}, f32[4]{0:T(128)}, u32[]{:S(2)}) copy-start(f32[4]{0:T(128)} %get-tuple-element.48) | copy-start | bytes 52
  540.5 52.0 %copy-start.24 = (f32[17]{0:T(128)S(1)}, f32[17]{0:T(128)}, u32[]{:S(2)}) copy-start(f32[17]{0:T(128)} %add_convert_fusion.3) | copy-start | bytes 208
  641.7 47.2 %collective-permute-start.11 = (f32[2048,256]{1,0:T(8,128)}, f32[2048,256]{1,0:T(8,128)}, u32[]{:S(2)}, u32[]{:S(2)}) collective-permute-start(f32[2048,256]{1,0:T(8,128)} %copy.171), channel_id=1, source_target_pairs={{0,1},{1,0},{2,3},{3,2},{4,5},{5,4},{6,7},{7,6},{8,9},{9,8},{10,11... | collective-permute-start | bytes 6291464 | tf_op jit(solution)/shard_map/ppermute | solution.py:56
  643.2 49.5 %copy-start.1 = (f32[16,128,128]{2,1,0:T(8,128)S(1)}, f32[16,128,128]{2,1,0:T(8,128)}, u32[]{:S(2)}) copy-start(f32[16,128,128]{2,1,0:T(8,128)} %param.6) | copy-start | bytes 3145732
  (8 other events, 31.2 us)
